TPU v7x, 32 devices: a whole 2x2x4 slice. The times are simulated.
32 devices in a mesh: grp: 4 (over x, core), tp: 4 (over z), cores: 2 (over y).
Axes of the slice: x: 2, y: 2, z: 4, core: 2. Of those that a mesh axis runs over, the one named last changes fastest.
Arguments:
- tokens: bfloat16 [4096, 8192], P('grp', ('tp', 'cores')), may hold values from -6 to 6
- gate_up_weight: bfloat16 [8192, 2, 16384], P(None, None, ('tp', 'cores')), may hold values from -0.0625 to 0.0625
- down_factor_pool: bfloat16 [8, 8192, 256], P(('tp', 'cores'), 'grp'), may hold values from -0.0625 to 0.0625
- up_factor_pool: bfloat16 [8, 4, 8, 128, 1024], P(('tp', 'cores'), 'grp'), may hold values from -0.5 to 0.5
- segment_adapters: int32 [4, 3], replicated, may hold values from 0 to 7
- segment_tile_counts: int32 [4, 3], P('grp'), may hold values from 1 to 4, 8 in all within a row
- adapter_pool_rows: int32 [8], replicated, may hold values from 0 to 7, each once
Outputs:
- hidden: bfloat16 [4096, 16384], P('grp', ('tp', 'cores'))
Inputs may be any that keep to these rules, and one draw needn't show every extreme that they name: `segment_tile_counts`: each row sums to 8. `adapter_pool_rows`: each pool row appears once.
All inputs are finite; a program needn't handle non-finite values.
Results may differ from a plain program's by a relative error of at most 0.0036.
Values may be sent and summed in bfloat16 or wider, within the bound.
A program may use at most 320 MiB of HBM per device.

v0:
```python
import jax
import jax.numpy as jnp
from jax import lax
from jax.sharding import PartitionSpec as P

TILE = 128
adapter_scale = 0.5


def tile_segments(tile_lengths, tile_count):
    bounds = jnp.cumsum(tile_lengths)
    positions = jnp.arange(tile_count, dtype=jnp.int32)
    return jnp.sum((bounds[None, :] <= positions[:, None]).astype(jnp.int32), axis=1)


def per_device(
    tokens,
    gate_up_weight,
    down_factor_pool,
    up_factor_pool,
    segment_adapters,
    segment_tile_counts,
    adapter_pool_rows,
):
    groups = lax.axis_size("grp")
    device_shares = lax.axis_size(("tp", "cores"))
    piece_index = lax.axis_index(("tp", "cores"))
    token_count = tokens.shape[0]
    full_width = tokens.shape[1] * device_shares
    local_hidden_width = gate_up_weight.shape[2]
    twice_rank = down_factor_pool.shape[2]
    rank_size = twice_rank // 2
    share_rows = down_factor_pool.shape[1] // device_shares
    local_count = down_factor_pool.shape[0]
    seg_count = segment_adapters.shape[1]
    narrow = local_hidden_width // groups
    local_down_factor = down_factor_pool.reshape(
        local_count, device_shares, share_rows * twice_rank
    )
    local_up_factor = up_factor_pool.reshape(local_count, device_shares, -1)
    a_spread, b_spread = (
        lax.all_to_all(local_down_factor, ("tp", "cores"), split_axis=1, concat_axis=0, tiled=True),
        lax.all_to_all(local_up_factor, ("tp", "cores"), split_axis=1, concat_axis=0, tiled=True),
    )
    all_slots = jnp.take(adapter_pool_rows, segment_adapters)
    a_wanted = jnp.take(a_spread, all_slots, axis=0)
    b_wanted = jnp.take(b_spread, all_slots, axis=0)
    a_arrived, b_arrived = (
        lax.all_to_all(a_wanted, "grp", split_axis=0, concat_axis=2, tiled=True),
        lax.all_to_all(b_wanted, "grp", split_axis=0, concat_axis=2, tiled=True),
    )
    a_chosen = a_arrived.reshape(seg_count, groups, -1)
    b_chosen = b_arrived.reshape(seg_count, groups, -1)
    gathered = lax.all_gather(tokens, ("tp", "cores"), axis=1, tiled=True)
    frozen_output = jnp.dot(
        gathered,
        gate_up_weight.reshape(full_width, 2 * local_hidden_width),
        preferred_element_type=jnp.float32,
    )
    frozen_output = frozen_output.reshape(token_count, 2, local_hidden_width)
    tile_count = token_count // TILE
    tile_seg = tile_segments(segment_tile_counts[0], tile_count)
    a_tiles = jnp.take(a_chosen, tile_seg, axis=0).reshape(
        tile_count, groups * share_rows, twice_rank
    )
    own_features = lax.dynamic_slice_in_dim(
        gathered.reshape(token_count, groups, device_shares, share_rows), piece_index, 1, axis=2
    )
    own_features = own_features.reshape(tile_count, TILE, groups * share_rows)
    partial_shrink = jnp.einsum(
        "tkd,tdr->tkr", own_features, a_tiles, preferred_element_type=jnp.float32
    )
    reduced_input = lax.psum(partial_shrink, ("tp", "cores")).astype(jnp.bfloat16)
    b_tiles = jnp.take(b_chosen, tile_seg, axis=0).reshape(tile_count, groups, rank_size, 2, narrow)
    gate_adapter_delta = jnp.einsum(
        "tkr,tmrw->tkmw",
        reduced_input[:, :, :rank_size],
        b_tiles[:, :, :, 0, :],
        preferred_element_type=jnp.float32,
    )
    up_adapter_delta = jnp.einsum(
        "tkr,tmrw->tkmw",
        reduced_input[:, :, rank_size:],
        b_tiles[:, :, :, 1, :],
        preferred_element_type=jnp.float32,
    )
    gate_combined = frozen_output[:, 0, :] + adapter_scale * gate_adapter_delta.reshape(
        token_count, local_hidden_width
    )
    up_combined = frozen_output[:, 1, :] + adapter_scale * up_adapter_delta.reshape(
        token_count, local_hidden_width
    )
    return (jax.nn.silu(gate_combined) * up_combined).astype(jnp.bfloat16)


def solution(mesh):
    return jax.shard_map(
        per_device,
        mesh=mesh,
        in_specs=(
            P("grp", ("tp", "cores")),
            P(None, None, ("tp", "cores")),
            P(("tp", "cores"), "grp", None),
            P(("tp", "cores"), "grp", None, None, None),
            P(),
            P("grp", None),
            P(),
        ),
        out_specs=P("grp", ("tp", "cores")),
        check_vma=False,
    )
```

profile of v0, /device:TPU:0, one launch (start us, length us, event | category | flops | bytes accessed | tf_op | source)
XLA Modules:
  0.0 634.1 jit_solution(12954752661760870075)
XLA Ops:
  11.1 7.3 %reduce.3 = bf16[8,65536]{1,0:T(8,128)(2,1)S(1)} reduce(bf16[8,1,65536]{2,1,0:T(2,128)(2,1)S(1)} %bitcast.106, bf16[]{:T(256)} %broadcast.154), dimensions={1}, to_apply=%bitcast.85.reduce_sub_computation | reduce | bytes 2097154
  20.3 7.5 %all-to-all-start = ((bf16[8,2,32768]{2,1,0:T(2,128)(2,1)}), bf16[8,2,32768]{2,1,0:T(2,128)(2,1)S(1)}, u32[]{:S(2)}, u32[]{:S(2)}) async-start(bf16[8,2,32768]{2,1,0:T(2,128)(2,1)} %reshape.206), calls=%async_computation | async-start | bytes 2097152 | tf_op jit(solution)/shard_map/all_to_all | solution.py:42
  32.9 13.0 %reduce.2 = bf16[8,131072]{1,0:T(8,128)(2,1)S(1)} reduce(bf16[8,1,131072]{2,1,0:T(2,128)(2,1)} %bitcast.100, bf16[]{:T(256)} %broadcast.154), dimensions={1}, to_apply=%bitcast.83.reduce_sub_computation | reduce | bytes 4194306
  49.1 4.4 all-to-all-done
  58.1 5.8 reshape.207
  77.6 28.9 %all-to-all-done.2 = bf16[8,2,65536]{2,1,0:T(2,128)(2,1)S(1)} async-done(((bf16[8,2,65536]{2,1,0:T(2,128)(2,1)}), bf16[8,2,65536]{2,1,0:T(2,128)(2,1)S(1)}, u32[]{:S(2)}, u32[]{:S(2)}) %all-to-all-start.2) | async-done | bytes 2097184 | tf_op jit(solution)/shard_map/all_to_all | solution.py:43
  106.5 4.7 all-to-all-start.1
  115.5 4.5 copy.79
  131.6 5.8 fusion.8
  137.3 5.0 all-to-all-start.3
  143.2 45.1 %copy.69 = bf16[1024,8,2,2048]{3,1,2,0:T(8,128)(2,1)} copy(bf16[1024,8,2,2048]{3,2,1,0:T(2,128)(2,1)} %bitcast.33) | data formatting | bytes 134217728
  188.3 83.4 %copy.48 = bf16[4096,8192]{1,0:T(8,128)(2,1)} copy(bf16[4096,8192]{0,1:T(8,128)(2,1)} %bitcast.1) | data formatting | bytes 134217728 | tf_op jit(solution)/shard_map/dot_general | solution.py:55
  274.9 5.4 gather_fusion.2
  280.3 7.9 %gather.27 = bf16[8,1024,256]{2,1,0:T(8,128)(2,1)} reshape(bf16[8,4,65536]{2,1,0:T(4,128)(2,1)} %gather_fusion.2) | data formatting | bytes 8388608 | tf_op jit(solution)/shard_map/jit(_take)/gather | solution.py:63
  288.3 5.2 copy.78
  294.5 5.4 gather_fusion.5
  299.9 5.5 gather_fusion.6
  305.4 8.3 %pad_maximum_fusion = bf16[8,4,131072]{2,1,0:T(4,128)(2,1)} fusion(bf16[8,4,65536]{2,1,0:T(4,128)(2,1)} %gather_fusion.6, bf16[8,4,65536]{2,1,0:T(4,128)(2,1)} %gather_fusion.5), kind=kLoop, calls=%fused_computation.15 | loop fusion | flops 16777216 | bytes 16777216
  313.8 12.5 %reshape.201 = bf16[8,4,128,2,512]{4,3,2,1,0:T(2,128)(2,1)} reshape(bf16[8,4,131072]{2,1,0:T(4,128)(2,1)} %pad_maximum_fusion) | data formatting | bytes 16777216 | tf_op jit(solution)/shard_map/jit(_take)/gather | solution.py:74
  326.3 8.2 %copy_select_fusion = bf16[8,4,128,2,512]{4,2,1,0,3:T(8,128)(2,1)} fusion(bf16[8,4,128,2,512]{4,3,2,1,0:T(2,128)(2,1)} %reshape.201, pred[8]{0:T(512)(128)(4,1)S(1)} %compare_and_fusion.1), kind=kLoop, calls=%fused_computation.16 | loop fusion | flops 4194304 | bytes 16777224 | tf_op jit(solution)/shard_map/jit(_take)/select_n | solution.py:74
  334.6 37.6 %all-gather.2.cloned.1.call-done = bf16[1024,8192]{1,0:T(8,128)(2,1)} async-done(((bf16[1024,1024]{1,0:T(8,128)(2,1)}), bf16[1024,8192]{1,0:T(8,128)(2,1)}) %all-gather.2.cloned.1.call-update) | async-done | bytes 16777232 | tf_op jit(solution)/shard_map/all_gather | solution.py:54
  372.2 10.3 %copy.70 = bf16[128,8,32,256]{3,2,1,0:T(8,128)(2,1)S(1)} copy(bf16[128,8,32,256]{3,1,2,0:T(8,128)(2,1)} %bitcast.102) | data formatting | bytes 33554432
  382.4 13.7 %dynamic-slice_reduce_fusion = bf16[1024,4,256]{2,1,0:T(4,128)(2,1)S(1)} fusion(bf16[1024,4,8,256]{3,2,1,0:T(8,128)(2,1)S(1)} %bitcast.98, s32[]{:T(128)S(6)} %select_n.80), kind=kLoop, calls=%fused_computation.27 | loop fusion | bytes 4194308 | tf_op jit(solution)/shard_map/dynamic_slice | solution.py:66
  402.6 70.0 %all-reduce.1 = bf16[8,128,256]{2,1,0:T(8,128)(2,1)S(1)} all-reduce(f32[8,128,256]{2,1,0:T(8,128)S(1)} %fusion.9), channel_id=1, replica_groups=mesh['grp'=4,'tp'=4,'cores'=2] {'tp','cores'}, use_global_device_ids=true, to_apply=%region_2.3 | all-reduce | flops 262144 | bytes 1572864 | tf_op jit(solution)/shard_map/psum | solution.py:73
  472.6 6.6 %broadcast_multiply_fusion.1 = f32[8,128,4,512]{3,1,2,0:T(8,128)} fusion(bf16[8,4,128,2,512]{4,2,1,0,3:T(8,128)(2,1)} %copy_select_fusion, bf16[8,128,256]{2,1,0:T(8,128)(2,1)S(1)} %all-reduce.1), kind=kOutput, calls=%fused_computation.24 | convolution fusion | flops 538968064 | bytes 12845056 | tf_op jit(solution)/shard_map/tkr,tmrw->tkmw/dot_general | solution.py:75
  479.2 6.6 %broadcast_multiply_fusion = f32[8,128,4,512]{3,1,2,0:T(8,128)} fusion(bf16[8,4,128,2,512]{4,2,1,0,3:T(8,128)(2,1)} %copy_select_fusion, bf16[8,128,256]{2,1,0:T(8,128)(2,1)S(1)} %all-reduce.1), kind=kOutput, calls=%fused_computation.23 | convolution fusion | flops 538968064 | bytes 12845056 | tf_op jit(solution)/shard_map/tkr,tmrw->tkmw/dot_general | solution.py:81
  485.8 12.1 %copy.60 = f32[8,128,4,512]{3,2,1,0:T(4,128)} copy(f32[8,128,4,512]{3,1,2,0:T(8,128)} %broadcast_multiply_fusion) | data formatting | bytes 16777216 | tf_op jit(solution)/shard_map/mul | solution.py:90
  497.9 11.1 %copy.72 = f32[128,8,4,512]{3,1,2,0:T(8,128)} copy(f32[128,8,4,512]{3,2,1,0:T(4,128)} %bitcast.94) | data formatting | bytes 16777216
  509.0 12.1 %copy.59 = f32[8,128,4,512]{3,2,1,0:T(4,128)} copy(f32[8,128,4,512]{3,1,2,0:T(8,128)} %broadcast_multiply_fusion.1) | data formatting | bytes 16777216 | tf_op jit(solution)/shard_map/mul | solution.py:87
  521.0 10.8 %copy.71 = f32[128,8,4,512]{3,1,2,0:T(8,128)} copy(f32[128,8,4,512]{3,2,1,0:T(4,128)} %bitcast.95) | data formatting | bytes 16777216
  531.8 80.5 %fusion = f32[1024,2,2048]{2,0,1:T(8,128)} fusion(bf16[2,2048,8192]{2,1,0:T(8,128)(2,1)} %bitcast.2, bf16[1024,8192]{1,0:T(8,128)(2,1)} %all-gather.2.cloned.1.call-done), kind=kOutput, calls=%fused_computation.7 | convolution fusion | flops 68719476736 | bytes 100663296 | tf_op jit(solution)/shard_map/dot_general | solution.py:55
  612.3 14.8 %fusion.4 = bf16[1024,2048]{1,0:T(8,128)(2,1)} fusion(f32[1024,2048]{1,0:T(8,128)} %bitcast.96, f32[1024,2,2048]{2,0,1:T(8,128)} %fusion, f32[1024,2048]{1,0:T(8,128)} %bitcast.97), kind=kLoop, calls=%fused_computation.12 | loop fusion | flops 16777216 | bytes 37748736 | tf_op jit(solution)/shard_map/convert_element_type | solution.py:93
  (49 shorter events, 60.6 us)
Async XLA Ops:
  6.5 21.4 %copy-start = (s32[8]{0:T(128)S(1)}, s32[8]{0:T(128)}, u32[]{:S(2)}) copy-start(s32[8]{0:T(128)} %param.13) | copy-start | bytes 100
  10.5 17.3 %copy-start.4 = (s32[4,3]{1,0:T(4,128)S(1)}, s32[4,3]{1,0:T(4,128)}, u32[]{:S(2)}) copy-start(s32[4,3]{1,0:T(4,128)} %param.11) | copy-start | bytes 148
  18.4 10.4 %copy-start.3 = (bf16[1,1,8,128,1024]{4,3,2,1,0:T(8,128)(2,1)S(1)}, bf16[1,1,8,128,1024]{4,3,2,1,0:T(8,128)(2,1)}, u32[]{:S(2)}) copy-start(bf16[1,1,8,128,1024]{4,3,2,1,0:T(8,128)(2,1)} %param.10) | copy-start | bytes 6291460
  20.3 33.2 %all-to-all-start = ((bf16[8,2,32768]{2,1,0:T(2,128)(2,1)}), bf16[8,2,32768]{2,1,0:T(2,128)(2,1)S(1)}, u32[]{:S(2)}, u32[]{:S(2)}) async-start(bf16[8,2,32768]{2,1,0:T(2,128)(2,1)} %reshape.206), calls=%async_computation | async-start | bytes 2097152 | tf_op jit(solution)/shard_map/all_to_all | solution.py:42
  53.5 1.0 copy-start.2
  54.5 52.0 %all-to-all-start.2 = ((bf16[8,2,65536]{2,1,0:T(2,128)(2,1)}), bf16[8,2,65536]{2,1,0:T(2,128)(2,1)S(1)}, u32[]{:S(2)}, u32[]{:S(2)}) async-start(bf16[8,2,65536]{2,1,0:T(2,128)(2,1)} %reshape.204), calls=%async_computation.2 | async-start | bytes 4194304 | tf_op jit(solution)/shard_map/all_to_all | solution.py:43
  106.5 30.8 %all-to-all-start.1 = ((bf16[4,3,1,65536]{3,1,2,0:T(4,128)(2,1)}), bf16[4,3,1,65536]{3,1,2,0:T(4,128)(2,1)}, u32[]{:S(2)}, u32[]{:S(2)}) async-start(bf16[4,3,1,65536]{3,1,2,0:T(4,128)(2,1)} %select_bitcast_fusion), calls=%async_computation.1 | async-start | bytes 4194304 | tf_op jit(solution)/shard_map/all_to_all | solution.py:49
  137.3 5.7 copy-start.5
  137.3 150.9 %all-to-all-start.3 = ((bf16[4,3,1,131072]{3,1,2,0:T(4,128)(2,1)}), bf16[4,3,1,131072]{3,1,2,0:T(4,128)(2,1)}, u32[]{:S(2)}, u32[]{:S(2)}) async-start(bf16[4,3,1,131072]{3,1,2,0:T(4,128)(2,1)} %fusion.8), calls=%async_computation.3 | async-start | bytes 8388608 | tf_op jit(solution)/shard_map/all_to_all | solution.py:50
  142.3 229.8 %all-gather.2.cloned.1.call-start = ((), (), s32[]{:S(2)}) async-start(), calls=%async_computation.4 | async-start | bytes 18874368 | tf_op jit(solution)/shard_map/all_gather | solution.py:54
  612.3 14.8 %copy-start.1 = (s32[8]{0:T(128)S(1)}, s32[8]{0:T(128)}, u32[]{:S(2)}) copy-start(s32[8]{0:T(128)} %param.13) | copy-start | bytes 100
Sparse Core Ops, SparseCore 0:
  145.3 226.8 all-gather.1
where the time goes:
time: 644 us; the launch traced here: 634 us
  local copies, waits for them, and re-layouts  299 us (46%)
  matrix products  97.5 us (15%)
  waiting for transfers between devices  71.2 us (11%)
  blocking collectives  70 us (11%)
  other arithmetic  61.6 us (10%)
  starting transfers between devices  21.2 us (3%)
  between operations  13.8 us (2%)
    unnamed x23, local copies, waits for them, and re-layouts  101 us
    dot_general x1, local copies, waits for them, and re-layouts, per_device(): jnp.dot(gathered, gate_up_weight.reshape(full_width, 2 * local_hidden_wid...  83.4 us
    dot_general x1, matrix products, per_device(): jnp.dot(gathered, gate_up_weight.reshape(full_width, 2 * local_hidden_wid...  80.5 us
    psum x1, blocking collectives, per_device(): lax.psum(partial_shrink, ('tp', 'cores')).astype(jnp.bfloat16)  70 us
    all_gather x1, waiting for transfers between devices, per_device(): gathered = lax.all_gather(tokens, ('tp', 'cores'), axis=1, tiled=True)  37.6 us
    all_to_all x1, waiting for transfers between devices, per_device(): lax.all_to_all(local_up_factor, ('tp', 'cores'), split_axis=1, concat_axi...  28.9 us
    unnamed x3, other arithmetic  28.6 us
    gather x4, local copies, waits for them, and re-layouts, per_device(): jnp.take(b_chosen, tile_seg, axis=0)  24.6 us
  transfers between devices with their start and end apart: 5, of which 3 were waited for; matrix products, arithmetic and copies ran while one was open for 41% of the time, Pallas kernels for 0%

commit v1 on v0

--- a/solution.py
+++ b/solution.py
@@ -5,6 +5,12 @@
 
 TILE = 128
 adapter_scale = 0.5
+
+
+def add_all(x, mesh_axis):
+    parts = lax.all_gather(x, mesh_axis, axis=0, tiled=False)
+    acc = parts.sum(axis=0)
+    return acc
 
 
 def tile_segments(tile_lengths, tile_count):
@@ -70,7 +76,7 @@
     partial_shrink = jnp.einsum(
         "tkd,tdr->tkr", own_features, a_tiles, preferred_element_type=jnp.float32
     )
-    reduced_input = lax.psum(partial_shrink, ("tp", "cores")).astype(jnp.bfloat16)
+    reduced_input = add_all(partial_shrink, ("tp", "cores")).astype(jnp.bfloat16)
     b_tiles = jnp.take(b_chosen, tile_seg, axis=0).reshape(tile_count, groups, rank_size, 2, narrow)
     gate_adapter_delta = jnp.einsum(
         "tkr,tmrw->tkmw",

time: 644 us -> 611 us (0.949)
  blocking collectives: 70 us -> 0 us
  waiting for transfers between devices: 71.2 us -> 105 us
    psum x1 -> x0, blocking collectives: 70 us -> none  [per_device(): lax.psum(partial_shrink, ('tp', 'cores')).astype(jnp.bfloat16)]
    all_to_all x1, waiting for transfers between devices: 28.9 us -> 69.2 us  [per_device(): lax.all_to_all(local_up_factor, ('tp', 'cores'), split_axis=1, concat_axi...]
    all_gather x1, waiting for transfers between devices: 37.6 us -> 0.01 us  [per_device(): gathered = lax.all_gather(tokens, ('tp', 'cores'), axis=1, tiled=True)]
    all_to_all x1, waiting for transfers between devices: 4.43 us -> 21.3 us  [per_device(): lax.all_to_all(local_down_factor, ('tp', 'cores'), split_axis=1, concat_a...]
    all_gather x0 -> x1, waiting for transfers between devices: none -> 13.9 us  [add_all(): parts = lax.all_gather(x, mesh_axis, axis=0, tiled=False)]
    unnamed x23 -> x27, local copies, waits for them, and re-layouts: 101 us -> 101 us
    unnamed x3 -> x4, other arithmetic: 28.6 us -> 28.7 us
  transfers between devices with their start and end apart: 5 -> 6, of which waited for: 3 -> 3; matrix products, arithmetic and copies ran while one was open for 41% -> 56% of each run, Pallas kernels for 0% -> 0%
where the time goes in v1:
time: 611 us; the launch traced here: 601 us
  local copies, waits for them, and re-layouts  299 us (49%)
  waiting for transfers between devices  105 us (17%)
  matrix products  99.1 us (16%)
  other arithmetic  63.3 us (10%)
  starting transfers between devices  21.2 us (3%)
  between operations  13.8 us (2%)
    unnamed x27, local copies, waits for them, and re-layouts  101 us
    dot_general x1, local copies, waits for them, and re-layouts, per_device(): jnp.dot(gathered, gate_up_weight.reshape(full_width, 2 * local_hidden_wid...  83.7 us
    dot_general x1, matrix products, per_device(): jnp.dot(gathered, gate_up_weight.reshape(full_width, 2 * local_hidden_wid...  81 us
    all_to_all x1, waiting for transfers between devices, per_device(): lax.all_to_all(local_up_factor, ('tp', 'cores'), split_axis=1, concat_axi...  69.2 us
    unnamed x4, other arithmetic  28.7 us
    gather x4, local copies, waits for them, and re-layouts, per_device(): jnp.take(b_chosen, tile_seg, axis=0)  24.6 us
    all_to_all x1, waiting for transfers between devices, per_device(): lax.all_to_all(local_down_factor, ('tp', 'cores'), split_axis=1, concat_a...  21.3 us
    all_gather x1, waiting for transfers between devices, add_all(): parts = lax.all_gather(x, mesh_axis, axis=0, tiled=False)  13.9 us
  transfers between devices with their start and end apart: 6, of which 3 were waited for; matrix products, arithmetic and copies ran while one was open for 56% of the time, Pallas kernels for 0%

profile of v1, /device:TPU:0, one launch (start us, length us, event | category | flops | bytes accessed | tf_op | source)
XLA Modules:
  0.0 601.0 jit_solution(11660585580552339724)
XLA Ops:
  11.1 7.3 %reduce.3 = bf16[8,65536]{1,0:T(8,128)(2,1)S(1)} reduce(bf16[8,1,65536]{2,1,0:T(2,128)(2,1)S(1)} %bitcast.110, bf16[]{:T(256)} %broadcast.154), dimensions={1}, to_apply=%bitcast.86.reduce_sub_computation | reduce | bytes 2097154
  20.2 7.3 %all-to-all-start = ((bf16[8,2,32768]{2,1,0:T(2,128)(2,1)}), bf16[8,2,32768]{2,1,0:T(2,128)(2,1)S(1)}, u32[]{:S(2)}, u32[]{:S(2)}) async-start(bf16[8,2,32768]{2,1,0:T(2,128)(2,1)} %reshape.207), calls=%async_computation | async-start | bytes 2097152 | tf_op jit(solution)/shard_map/all_to_all | solution.py:48
  33.4 13.0 %reduce.2 = bf16[8,131072]{1,0:T(8,128)(2,1)S(1)} reduce(bf16[8,1,131072]{2,1,0:T(2,128)(2,1)} %bitcast.103, bf16[]{:T(256)} %broadcast.154), dimensions={1}, to_apply=%bitcast.84.reduce_sub_computation | reduce | bytes 4194306
  49.5 21.3 %all-to-all-done = bf16[8,2,32768]{2,1,0:T(2,128)(2,1)S(1)} async-done(((bf16[8,2,32768]{2,1,0:T(2,128)(2,1)}), bf16[8,2,32768]{2,1,0:T(2,128)(2,1)S(1)}, u32[]{:S(2)}, u32[]{:S(2)}) %all-to-all-start) | async-done | bytes 1048608 | tf_op jit(solution)/shard_map/all_to_all | solution.py:48
  75.4 5.8 reshape.208
  95.0 69.2 %all-to-all-done.2 = bf16[8,2,65536]{2,1,0:T(2,128)(2,1)S(1)} async-done(((bf16[8,2,65536]{2,1,0:T(2,128)(2,1)}), bf16[8,2,65536]{2,1,0:T(2,128)(2,1)S(1)}, u32[]{:S(2)}, u32[]{:S(2)}) %all-to-all-start.2) | async-done | bytes 2097184 | tf_op jit(solution)/shard_map/all_to_all | solution.py:49
  164.2 4.7 all-to-all-start.1
  173.2 4.9 copy.79
  189.7 5.8 fusion.8
  195.4 5.0 all-to-all-start.3
  201.1 44.3 %copy.69 = bf16[1024,8,2,2048]{3,1,2,0:T(8,128)(2,1)} copy(bf16[1024,8,2,2048]{3,2,1,0:T(2,128)(2,1)} %bitcast.34) | data formatting | bytes 134217728
  245.4 83.7 %copy.48 = bf16[4096,8192]{1,0:T(8,128)(2,1)} copy(bf16[4096,8192]{0,1:T(8,128)(2,1)} %bitcast.1) | data formatting | bytes 134217728 | tf_op jit(solution)/shard_map/dot_general | solution.py:61
  332.3 5.4 gather_fusion.2
  337.6 7.9 %gather.27 = bf16[8,1024,256]{2,1,0:T(8,128)(2,1)} reshape(bf16[8,4,65536]{2,1,0:T(4,128)(2,1)} %gather_fusion.2) | data formatting | bytes 8388608 | tf_op jit(solution)/shard_map/jit(_take)/gather | solution.py:69
  345.5 5.2 copy.78
  351.8 5.4 gather_fusion.5
  357.2 5.5 gather_fusion.6
  362.7 10.3 %copy.70 = bf16[128,8,32,256]{3,2,1,0:T(8,128)(2,1)S(1)} copy(bf16[128,8,32,256]{3,1,2,0:T(8,128)(2,1)} %bitcast.105) | data formatting | bytes 33554432
  373.0 13.7 %dynamic-slice_reduce_fusion = bf16[1024,4,256]{2,1,0:T(4,128)(2,1)S(1)} fusion(bf16[1024,4,8,256]{3,2,1,0:T(8,128)(2,1)S(1)} %bitcast.101, s32[]{:T(128)S(6)} %select_n.80), kind=kLoop, calls=%fused_computation.27 | loop fusion | bytes 4194308 | tf_op jit(solution)/shard_map/dynamic_slice | solution.py:72
  389.4 4.8 fusion.9
  394.2 8.4 %pad_maximum_fusion = bf16[8,4,131072]{2,1,0:T(4,128)(2,1)} fusion(bf16[8,4,65536]{2,1,0:T(4,128)(2,1)} %gather_fusion.6, bf16[8,4,65536]{2,1,0:T(4,128)(2,1)} %gather_fusion.5), kind=kLoop, calls=%fused_computation.15 | loop fusion | flops 16777216 | bytes 16777216
  402.6 12.6 %reshape.202 = bf16[8,4,128,2,512]{4,3,2,1,0:T(2,128)(2,1)} reshape(bf16[8,4,131072]{2,1,0:T(4,128)(2,1)} %pad_maximum_fusion) | data formatting | bytes 16777216 | tf_op jit(solution)/shard_map/jit(_take)/gather | solution.py:80
  415.2 8.2 %copy_select_fusion = bf16[8,4,128,2,512]{4,2,1,0,3:T(8,128)(2,1)} fusion(bf16[8,4,128,2,512]{4,3,2,1,0:T(2,128)(2,1)} %reshape.202, pred[8]{0:T(512)(128)(4,1)S(1)} %compare_and_fusion.1), kind=kLoop, calls=%fused_computation.16 | loop fusion | flops 4194304 | bytes 16777224 | tf_op jit(solution)/shard_map/jit(_take)/select_n | solution.py:80
  423.4 81.0 %fusion = f32[1024,2,2048]{2,0,1:T(8,128)} fusion(bf16[2,2048,8192]{2,1,0:T(8,128)(2,1)} %bitcast.2, bf16[1024,8192]{1,0:T(8,128)(2,1)} %all-gather.4.cloned.1.call-done), kind=kOutput, calls=%fused_computation.7 | convolution fusion | flops 68719476736 | bytes 100663296 | tf_op jit(solution)/shard_map/dot_general | solution.py:61
  504.4 13.9 %all-gather.6.cloned.1.call-done = f32[64,128,256]{2,1,0:T(8,128)} async-done(((f32[8,128,256]{2,1,0:T(8,128)}), f32[64,128,256]{2,1,0:T(8,128)}) %all-gather.6.cloned.1.call-update) | async-done | bytes 8388624 | tf_op jit(solution)/shard_map/all_gather | solution.py:11
  522.4 6.7 %broadcast_multiply_fusion.1 = f32[8,128,4,512]{3,1,2,0:T(8,128)} fusion(bf16[8,4,128,2,512]{4,2,1,0,3:T(8,128)(2,1)} %copy_select_fusion, bf16[8,128,256]{2,1,0:T(8,128)(2,1)S(1)} %reduce_sum.22), kind=kOutput, calls=%fused_computation.24 | convolution fusion | flops 538968064 | bytes 12845056 | tf_op jit(solution)/shard_map/tkr,tmrw->tkmw/dot_general | solution.py:81
  529.0 6.7 %broadcast_multiply_fusion = f32[8,128,4,512]{3,1,2,0:T(8,128)} fusion(bf16[8,4,128,2,512]{4,2,1,0,3:T(8,128)(2,1)} %copy_select_fusion, bf16[8,128,256]{2,1,0:T(8,128)(2,1)S(1)} %reduce_sum.22), kind=kOutput, calls=%fused_computation.23 | convolution fusion | flops 538968064 | bytes 12845056 | tf_op jit(solution)/shard_map/tkr,tmrw->tkmw/dot_general | solution.py:87
  535.7 12.0 %copy.60 = f32[8,128,4,512]{3,2,1,0:T(4,128)} copy(f32[8,128,4,512]{3,1,2,0:T(8,128)} %broadcast_multiply_fusion) | data formatting | bytes 16777216 | tf_op jit(solution)/shard_map/mul | solution.py:96
  547.7 10.9 %copy.72 = f32[128,8,4,512]{3,1,2,0:T(8,128)} copy(f32[128,8,4,512]{3,2,1,0:T(4,128)} %bitcast.95) | data formatting | bytes 16777216
  558.6 12.0 %copy.59 = f32[8,128,4,512]{3,2,1,0:T(4,128)} copy(f32[8,128,4,512]{3,1,2,0:T(8,128)} %broadcast_multiply_fusion.1) | data formatting | bytes 16777216 | tf_op jit(solution)/shard_map/mul | solution.py:93
  570.6 11.0 %copy.71 = f32[128,8,4,512]{3,1,2,0:T(8,128)} copy(f32[128,8,4,512]{3,2,1,0:T(4,128)} %bitcast.96) | data formatting | bytes 16777216
  581.6 12.4 %fusion.4 = bf16[1024,2048]{1,0:T(8,128)(2,1)} fusion(f32[1024,2048]{1,0:T(8,128)S(1)} %bitcast.99, f32[1024,2,2048]{2,0,1:T(8,128)} %fusion, f32[1024,2048]{1,0:T(8,128)} %bitcast.100), kind=kLoop, calls=%fused_computation.12 | loop fusion | flops 16777216 | bytes 37748736 | tf_op jit(solution)/shard_map/convert_element_type | solution.py:99
  (57 shorter events, 61.3 us)
Async XLA Ops:
  6.5 21.8 %copy-start = (s32[8]{0:T(128)S(1)}, s32[8]{0:T(128)}, u32[]{:S(2)}) copy-start(s32[8]{0:T(128)} %param.13) | copy-start | bytes 100
  11.1 17.2 %copy-start.4 = (s32[4,3]{1,0:T(4,128)S(1)}, s32[4,3]{1,0:T(4,128)}, u32[]{:S(2)}) copy-start(s32[4,3]{1,0:T(4,128)} %param.11) | copy-start | bytes 148
  18.3 10.9 %copy-start.3 = (bf16[1,1,8,128,1024]{4,3,2,1,0:T(8,128)(2,1)S(1)}, bf16[1,1,8,128,1024]{4,3,2,1,0:T(8,128)(2,1)}, u32[]{:S(2)}) copy-start(bf16[1,1,8,128,1024]{4,3,2,1,0:T(8,128)(2,1)} %param.10) | copy-start | bytes 6291460
  20.2 50.6 %all-to-all-start = ((bf16[8,2,32768]{2,1,0:T(2,128)(2,1)}), bf16[8,2,32768]{2,1,0:T(2,128)(2,1)S(1)}, u32[]{:S(2)}, u32[]{:S(2)}) async-start(bf16[8,2,32768]{2,1,0:T(2,128)(2,1)} %reshape.207), calls=%async_computation | async-start | bytes 2097152 | tf_op jit(solution)/shard_map/all_to_all | solution.py:48
  27.5 335.2 %all-gather.4.cloned.1.call-start = ((), (), s32[]{:S(2)}) async-start(), calls=%async_computation.4 | async-start | bytes 18874368 | tf_op jit(solution)/shard_map/all_gather | solution.py:60
  70.8 1.0 copy-start.2
  71.8 92.4 %all-to-all-start.2 = ((bf16[8,2,65536]{2,1,0:T(2,128)(2,1)}), bf16[8,2,65536]{2,1,0:T(2,128)(2,1)S(1)}, u32[]{:S(2)}, u32[]{:S(2)}) async-start(bf16[8,2,65536]{2,1,0:T(2,128)(2,1)} %reshape.205), calls=%async_computation.2 | async-start | bytes 4194304 | tf_op jit(solution)/shard_map/all_to_all | solution.py:49
  164.2 31.2 %all-to-all-start.1 = ((bf16[4,3,1,65536]{3,1,2,0:T(4,128)(2,1)}), bf16[4,3,1,65536]{3,1,2,0:T(4,128)(2,1)}, u32[]{:S(2)}, u32[]{:S(2)}) async-start(bf16[4,3,1,65536]{3,1,2,0:T(4,128)(2,1)} %select_bitcast_fusion), calls=%async_computation.1 | async-start | bytes 4194304 | tf_op jit(solution)/shard_map/all_to_all | solution.py:55
  195.4 5.5 copy-start.5
  195.4 150.1 %all-to-all-start.3 = ((bf16[4,3,1,131072]{3,1,2,0:T(4,128)(2,1)}), bf16[4,3,1,131072]{3,1,2,0:T(4,128)(2,1)}, u32[]{:S(2)}, u32[]{:S(2)}) async-start(bf16[4,3,1,131072]{3,1,2,0:T(4,128)(2,1)} %fusion.8), calls=%async_computation.3 | async-start | bytes 8388608 | tf_op jit(solution)/shard_map/all_to_all | solution.py:56
  200.4 317.9 %all-gather.6.cloned.1.call-start = ((), (), s32[]{:S(2)}) async-start(), calls=%async_computation.5 | async-start | bytes 9437184 | tf_op jit(solution)/shard_map/all_gather | solution.py:11
  570.6 11.0 %slice-start = ((s8[8388608]{0:T(1024)(128)(4,1)}), s8[4194304]{0:T(1024)(128)(4,1)S(1)}, s32[]{:S(2)}) async-start(s8[8388608]{0:T(1024)(128)(4,1)} %bitcast.97), calls=%async_computation.6 | async-start | bytes 8388608
  570.6 11.0 %slice-start.1 = ((s8[8388608]{0:T(1024)(128)(4,1)}), s8[4194304]{0:T(1024)(128)(4,1)S(1)}, s32[]{:S(2)}) async-start(s8[8388608]{0:T(1024)(128)(4,1)} %bitcast.97), calls=%async_computation.7 | async-start | bytes 8388608
  581.6 12.4 %copy-start.1 = (s32[8]{0:T(128)S(1)}, s32[8]{0:T(128)}, u32[]{:S(2)}) copy-start(s32[8]{0:T(128)} %param.13) | copy-start | bytes 100
Sparse Core Ops, SparseCore 0:
  30.5 280.7 all-gather.3
  394.3 123.9 all-gather.5
